TPU v7x, 32 devices: a whole 2x2x4 slice. The times are simulated.
32 devices in a mesh: space: 16 (over z, x, core), chan: 2 (over y).
Axes of the slice: x: 2, y: 2, z: 4, core: 2. Of those that a mesh axis runs over, the one named last changes fastest.
Arguments:
- volume: bfloat16 [256, 16, 8, 128], P('chan', 'space'), may hold values from -6 to 6
- w_first: bfloat16 [256, 27, 256], P(None, None, 'chan'), may hold values from -0.078125 to 0.078125
- b_first: float32 [256], P('chan'), may hold values from -1.8 to 1.8
- w_second: bfloat16 [256, 27, 256], P('chan'), may hold values from -0.125 to 0.125
- b_second: float32 [256], P('chan'), may hold values from -1.8 to 1.8
Outputs:
- result: bfloat16 [256, 16, 8, 128], P('chan', 'space')
All inputs are finite; a program needn't handle non-finite values.
Results may differ from a plain program's by a relative error of at most 0.011.
Values may be sent and summed in bfloat16 or wider, within the bound.
No kernel may reach another device: no remote copies, remote signals or barrier semaphores. Data moves between devices by JAX's collectives and lax.ppermute only.
A program may use at most 64 MiB of HBM per device.

v0:
```python
import jax
import jax.numpy as jnp
from jax import lax
from jax.sharding import PartitionSpec as P


def with_halo(cells, sides, width):
    for axis, dim in sides:
        count = lax.axis_size(axis)
        ends = count - 1
        head = lax.slice_in_dim(cells, 0, width, axis=dim)
        tail = lax.slice_in_dim(cells, cells.shape[dim] - width, cells.shape[dim], axis=dim)
        cells = jnp.concatenate(
            [
                lax.ppermute(tail, axis, [(i, (i + 1) % count) for i in range(ends)]),
                cells,
                lax.ppermute(head, axis, [((i + 1) % count, i) for i in range(ends)]),
            ],
            axis=dim,
        )
    return cells


def apply_taps(slab, weights, row_pad):
    kernel = weights.reshape(weights.shape[0], 3, 3, 3, weights.shape[2])
    summed = lax.conv_general_dilated(
        slab[None],
        kernel,
        (1, 1, 1),
        [(0, 0), (row_pad, row_pad), (1, 1)],
        dimension_numbers=("NCDHW", "IDHWO", "NCDHW"),
        preferred_element_type=jnp.float32,
    )
    return summed[0]


def per_device(volume, w_first, b_first, w_second, b_second):
    gathered = lax.all_gather(volume, "chan", axis=0, tiled=True)
    framed = with_halo(gathered, (("space", 1),), 1)
    first_sum = apply_taps(framed, w_first, 1)
    hidden = jax.nn.relu(first_sum + b_first[:, None, None, None]).astype(jnp.bfloat16)
    beside_all = with_halo(hidden, (("space", 1),), 1)
    second_sum = lax.psum_scatter(
        apply_taps(beside_all, w_second, 1).astype(jnp.bfloat16),
        "chan",
        scatter_dimension=0,
        tiled=True,
    ).astype(jnp.float32)
    return jax.nn.relu(second_sum + b_second[:, None, None, None]).astype(jnp.bfloat16)


def solution(mesh):
    in_specs = (
        P("chan", "space", None, None),
        P(None, None, "chan"),
        P("chan"),
        P("chan", None, None),
        P("chan"),
    )
    out_specs = P("chan", "space", None, None)
    return jax.shard_map(
        per_device, mesh=mesh, in_specs=in_specs, out_specs=out_specs, check_vma=False
    )
```

profile of v0, /device:TPU:0, one launch (start us, length us, event | category | flops | bytes accessed | tf_op | source)
XLA Modules:
  0.0 113.9 jit_solution(8084966245108863844)
XLA Ops:
  6.5 0.0 copy-start
  6.5 0.0 reduce-scatter.4.cloned.1.call-start
  6.5 1.3 %copy.15 = bf16[128,1,8,128]{0,2,3,1:T(8,128)(2,1)S(1)} copy(bf16[128,1,8,128]{3,2,1,0:T(8,128)(2,1)} %param.5) | data formatting | bytes 524288 | tf_op args[0]
  7.9 10.0 %all_gather.3 = bf16[256,1,8,128]{0,2,3,1:T(8,128)(2,1)S(1)} all-gather(bf16[128,1,8,128]{0,2,3,1:T(8,128)(2,1)S(1)} %copy.15), channel_id=1, replica_groups=mesh['space'=16,'chan'=2] {'chan'}, dimensions={0}, use_global_device_ids=true | all-gather | bytes 786432 | tf_op jit(solution)/shard_map/all_gather | solution.py:38
  17.9 1.3 %collective-permute-start.1 = (bf16[256,1,8,128]{0,2,3,1:T(8,128)(2,1)S(1)}, bf16[256,1,8,128]{0,2,3,1:T(8,128)(2,1)S(1)}, u32[]{:S(2)}, u32[]{:S(2)}) collective-permute-start(bf16[256,1,8,128]{0,2,3,1:T(8,128)(2,1)S(1)} %all_gather.3), channel_id=1, source_target_pairs={{2,0},{4,2},{6,4},{8,6},{10,8},{12,10},{14,12},{16,14},{18,16},{20... | collective-permute-start | bytes 1572872 | tf_op jit(solution)/shard_map/ppermute | solution.py:17
  19.2 3.1 %collective-permute-start = (bf16[256,1,8,128]{0,2,3,1:T(8,128)(2,1)S(1)}, bf16[256,1,8,128]{0,2,3,1:T(8,128)(2,1)S(1)}, u32[]{:S(2)}, u32[]{:S(2)}) collective-permute-start(bf16[256,1,8,128]{0,2,3,1:T(8,128)(2,1)S(1)} %all_gather.3), channel_id=1, source_target_pairs={{0,2},{2,4},{4,6},{6,8},{8,10},{10,12},{12,14},{14,16},{16,18},{18... | collective-permute-start | bytes 1572872 | tf_op jit(solution)/shard_map/ppermute | solution.py:15
  22.2 0.0 collective-permute-done.1
  22.2 1.5 %collective-permute-done = bf16[256,1,8,128]{0,2,3,1:T(8,128)(2,1)S(1)} collective-permute-done((bf16[256,1,8,128]{0,2,3,1:T(8,128)(2,1)S(1)}, bf16[256,1,8,128]{0,2,3,1:T(8,128)(2,1)S(1)}, u32[]{:S(2)}, u32[]{:S(2)}) %collective-permute-start) | collective-permute-done | bytes 524320 | tf_op jit(solution)/shard_map/ppermute | solution.py:15
  23.7 0.2 maximum_bitcast_fusion
  23.9 0.1 pad
  24.0 0.0 copy-start.3
  24.0 0.0 copy-start.4
  24.0 0.3 copy.17
  24.4 1.1 copy-done.3
  25.5 0.0 copy-done.4
  25.5 0.0 copy-start.2
  25.5 4.1 %fusion.10 = f32[1,8,8,17,128]{4,2,3,1,0:T(8,128)S(1)} fusion(bf16[256,3,3,3,128]{4,0,3,2,1:T(8,128)(2,1)S(1)} %bitcast.46, bf16[256,3,8,1,7,2]{0,4,5,2,1,3:T(8,128)(2,1)S(1)} %slice.4, bf16[256,3,8,1,8,17]{0,4,5,2,1,3:T(8,128)(2,1)S(1)} %copy.17, pred[8,17]{0,1:T(8,128)(4,1)S(1)} %copy-done.4), kind=kOutput, calls=%fused_computation.13 | convolution fusion | flops 1770496000 | bytes 4169864 | tf_op jit(solution)/shard_map/conv_general_dilated | solution.py:26
  29.6 0.1 copy.18
  29.7 0.0 copy-done.2
  29.7 0.1 fusion.22
  29.8 1.3 %collective-permute-start.3 = (bf16[128,1,8,128]{0,2,3,1:T(8,128)(2,1)S(1)}, bf16[128,1,8,128]{0,2,3,1:T(8,128)(2,1)S(1)}, u32[]{:S(2)}, u32[]{:S(2)}) collective-permute-start(bf16[128,1,8,128]{0,2,3,1:T(8,128)(2,1)S(1)} %fusion.22), channel_id=1, source_target_pairs={{2,0},{4,2},{6,4},{8,6},{10,8},{12,10},{14,12},{16,14},{18,16},{20... | collective-permute-start | bytes 786440 | tf_op jit(solution)/shard_map/ppermute | solution.py:17
  31.1 12.4 %collective-permute-start.2 = (bf16[128,1,8,128]{0,2,3,1:T(8,128)(2,1)S(1)}, bf16[128,1,8,128]{0,2,3,1:T(8,128)(2,1)S(1)}, u32[]{:S(2)}, u32[]{:S(2)}) collective-permute-start(bf16[128,1,8,128]{0,2,3,1:T(8,128)(2,1)S(1)} %fusion.22), channel_id=1, source_target_pairs={{0,2},{2,4},{4,6},{6,8},{8,10},{10,12},{12,14},{14,16},{16,18},{18... | collective-permute-start | bytes 786440 | tf_op jit(solution)/shard_map/ppermute | solution.py:15
  43.5 0.0 collective-permute-done.3
  43.5 0.9 collective-permute-done.2
  44.5 0.1 maximum_bitcast_fusion.1
  44.6 0.1 pad.2
  44.6 0.1 copy.20
  44.8 0.0 copy-done
  44.8 2.2 %fusion.9 = bf16[1,8,8,17,256]{4,2,3,1,0:T(8,128)(2,1)S(1)} fusion(bf16[128,3,3,3,256]{4,0,3,2,1:T(8,128)(2,1)S(1)} %bitcast.39, bf16[128,3,8,1,7,2]{0,4,5,2,1,3:T(8,128)(2,1)S(1)} %slice.6, bf16[128,3,8,1,8,17]{0,4,5,2,1,3:T(8,128)(2,1)S(1)} %copy.20, pred[8,17]{0,1:T(8,128)(4,1)S(1)} %copy-done.4), kind=kOutput, calls=%fused_computation.12 | convolution fusion | flops 1768112128 | bytes 3248264 | tf_op jit(solution)/shard_map/conv_general_dilated | solution.py:26
  47.0 0.1 copy.21
  47.1 11.8 %copy.23 = bf16[256,1,8,128]{2,3,1,0:T(8,128)(2,1)} copy(bf16[256,1,8,128]{0,2,3,1:T(8,128)(2,1)S(1)} %slice_bitcast_fusion) | data formatting | bytes 1048576
  58.9 13.5 %reshape.71 = bf16[256,1024]{1,0:T(8,128)(2,1)} reshape(bf16[256,1,128,8]{3,2,1,0:T(8,128)(2,1)} %bitcast.40) | data formatting | bytes 1048576
  72.4 0.0 reduce-scatter.4.cloned.1.call-update
  72.4 21.3 %reduce-scatter.4.cloned.1.call-done = bf16[128,1024]{1,0:T(8,128)(2,1)} async-done(((bf16[256,1024]{1,0:T(8,128)(2,1)}), bf16[128,1024]{1,0:T(8,128)(2,1)}) %reduce-scatter.4.cloned.1.call-update) | async-done | bytes 262160
  93.8 6.8 %reshape.72 = bf16[128,1,128,8]{3,2,1,0:T(8,128)(2,1)} reshape(bf16[128,1024]{1,0:T(8,128)(2,1)} %reduce-scatter.4.cloned.1.call-done) | data formatting | bytes 524288
  100.6 0.0 copy-start.1
  100.6 5.5 %copy.24 = bf16[128,1,8,128]{0,2,3,1:T(8,128)(2,1)S(1)} copy(bf16[128,1,8,128]{2,3,1,0:T(8,128)(2,1)} %bitcast.41) | data formatting | bytes 524288
  106.1 0.0 copy-done.1
  106.1 0.1 maximum_convert_fusion
  106.2 0.9 copy.22
  (3 shorter events, 0.1 us)
Async XLA Ops:
  6.5 38.3 %copy-start = (bf16[128,27,256]{2,0,1:T(8,128)(2,1)S(1)}, bf16[128,27,256]{2,0,1:T(8,128)(2,1)}, u32[]{:S(2)}) copy-start(bf16[128,27,256]{2,0,1:T(8,128)(2,1)} %param.8) | copy-start | bytes 5308420
  6.5 87.2 %reduce-scatter.4.cloned.1.call-start = ((), (), s32[]{:S(2)}) async-start(), calls=%async_computation.1 | async-start | bytes 786432
  17.9 4.4 %collective-permute-start.1 = (bf16[256,1,8,128]{0,2,3,1:T(8,128)(2,1)S(1)}, bf16[256,1,8,128]{0,2,3,1:T(8,128)(2,1)S(1)}, u32[]{:S(2)}, u32[]{:S(2)}) collective-permute-start(bf16[256,1,8,128]{0,2,3,1:T(8,128)(2,1)S(1)} %all_gather.3), channel_id=1, source_target_pairs={{2,0},{4,2},{6,4},{8,6},{10,8},{12,10},{14,12},{16,14},{18,16},{20... | collective-permute-start | bytes 1572872 | tf_op jit(solution)/shard_map/ppermute | solution.py:17
  19.2 4.6 %collective-permute-start = (bf16[256,1,8,128]{0,2,3,1:T(8,128)(2,1)S(1)}, bf16[256,1,8,128]{0,2,3,1:T(8,128)(2,1)S(1)}, u32[]{:S(2)}, u32[]{:S(2)}) collective-permute-start(bf16[256,1,8,128]{0,2,3,1:T(8,128)(2,1)S(1)} %all_gather.3), channel_id=1, source_target_pairs={{0,2},{2,4},{4,6},{6,8},{8,10},{10,12},{12,14},{14,16},{16,18},{18... | collective-permute-start | bytes 1572872 | tf_op jit(solution)/shard_map/ppermute | solution.py:15
  24.0 1.5 %copy-start.3 = (bf16[256,27,128]{2,0,1:T(8,128)(2,1)S(1)}, bf16[256,27,128]{2,0,1:T(8,128)(2,1)}, u32[]{:S(2)}) copy-start(bf16[256,27,128]{2,0,1:T(8,128)(2,1)} %param.6) | copy-start | bytes 5308420
  24.0 1.5 %copy-start.4 = (pred[8,17]{0,1:T(8,128)(4,1)S(1)}, pred[8,17]{0,1:T(8,128)(4,1)}, u32[]{:S(2)}) copy-start(pred[8,17]{0,1:T(8,128)(4,1)} %constant.13) | copy-start | bytes 412
  25.5 4.2 %copy-start.2 = (f32[128]{0:T(128)S(1)}, f32[128]{0:T(128)}, u32[]{:S(2)}) copy-start(f32[128]{0:T(128)} %param.7) | copy-start | bytes 1540
  29.8 13.7 %collective-permute-start.3 = (bf16[128,1,8,128]{0,2,3,1:T(8,128)(2,1)S(1)}, bf16[128,1,8,128]{0,2,3,1:T(8,128)(2,1)S(1)}, u32[]{:S(2)}, u32[]{:S(2)}) collective-permute-start(bf16[128,1,8,128]{0,2,3,1:T(8,128)(2,1)S(1)} %fusion.22), channel_id=1, source_target_pairs={{2,0},{4,2},{6,4},{8,6},{10,8},{12,10},{14,12},{16,14},{18,16},{20... | collective-permute-start | bytes 786440 | tf_op jit(solution)/shard_map/ppermute | solution.py:17
  31.1 13.4 %collective-permute-start.2 = (bf16[128,1,8,128]{0,2,3,1:T(8,128)(2,1)S(1)}, bf16[128,1,8,128]{0,2,3,1:T(8,128)(2,1)S(1)}, u32[]{:S(2)}, u32[]{:S(2)}) collective-permute-start(bf16[128,1,8,128]{0,2,3,1:T(8,128)(2,1)S(1)} %fusion.22), channel_id=1, source_target_pairs={{0,2},{2,4},{4,6},{6,8},{8,10},{10,12},{12,14},{14,16},{16,18},{18... | collective-permute-start | bytes 786440 | tf_op jit(solution)/shard_map/ppermute | solution.py:15
  100.6 5.5 %copy-start.1 = (f32[128]{0:T(128)S(1)}, f32[128]{0:T(128)}, u32[]{:S(2)}) copy-start(f32[128]{0:T(128)} %param.9) | copy-start | bytes 1540
Sparse Core Ops, SparseCore 0:
  72.5 21.1 reduce-scatter.3
where the time goes:
time: 114 us
  local copies, waits for them, and re-layouts  41.9 us (37%)
  waiting for transfers between devices  23.8 us (21%)
  starting transfers between devices  18.1 us (16%)
  between operations  13.6 us (12%)
  blocking collectives  9.98 us (9%)
  matrix products  6.29 us (6%)
    unnamed x15, local copies, waits for them, and re-layouts  40 us
    unnamed x2, waiting for transfers between devices  21.4 us
    ppermute x2, starting transfers between devices, with_halo(): lax.ppermute(tail, axis, [(i, (i + 1) % count) for i in range(ends)])  15.5 us
    all_gather x1, blocking collectives, per_device(): gathered = lax.all_gather(volume, 'chan', axis=0, tiled=True)  9.98 us
    conv_general_dilated x2, matrix products, apply_taps(): lax.conv_general_dilated(slab[None], kernel, (1, 1, 1), [(0, 0), (row_pad...  6.29 us
    ppermute x2, starting transfers between devices, with_halo(): lax.ppermute(head, axis, [((i + 1) % count, i) for i in range(ends)])  2.57 us
    ppermute x2, waiting for transfers between devices, with_halo(): lax.ppermute(tail, axis, [(i, (i + 1) % count) for i in range(ends)])  2.41 us
  transfers between devices with their start and end apart: 5, of which 3 were waited for; matrix products, arithmetic and copies ran while one was open for 0% of the time, Pallas kernels for 0%

commit v1 on v0

--- a/solution.py
+++ b/solution.py
@@ -35,7 +35,15 @@
 
 
 def per_device(volume, w_first, b_first, w_second, b_second):
-    gathered = lax.all_gather(volume, "chan", axis=0, tiled=True)
+    ways, here, step = (lax.axis_size("chan"), lax.axis_index("chan"), volume.shape[0])
+    line, have = (volume, 1)
+    while have < ways:
+        line = jnp.concatenate(
+            [line, lax.ppermute(line, "chan", [(d, (d - have) % ways) for d in range(ways)])],
+            axis=0,
+        )
+        have = 2 * have
+    gathered = jnp.roll(line, here * step, axis=0)
     framed = with_halo(gathered, (("space", 1),), 1)
     first_sum = apply_taps(framed, w_first, 1)
     hidden = jax.nn.relu(first_sum + b_first[:, None, None, None]).astype(jnp.bfloat16)

time: 114 us -> 114 us (level)
  blocking collectives: 9.98 us -> 0 us
  waiting for transfers between devices: 23.8 us -> 30.1 us
  starting transfers between devices: 18.1 us -> 21.1 us
    all_gather x1 -> x0, blocking collectives: 9.98 us -> none  [per_device(): gathered = lax.all_gather(volume, 'chan', axis=0, tiled=True)]
    ppermute x0 -> x1, waiting for transfers between devices: none -> 6.31 us  [per_device(): lax.ppermute(line, 'chan', [(d, (d - have) % ways) for d in range(ways)])]
    ppermute x0 -> x1, starting transfers between devices: none -> 3.03 us  [per_device(): lax.ppermute(line, 'chan', [(d, (d - have) % ways) for d in range(ways)])]
  transfers between devices with their start and end apart: 5 -> 6, of which waited for: 3 -> 4; matrix products, arithmetic and copies ran while one was open for 0% -> 0% of each run, Pallas kernels for 0% -> 0%
where the time goes in v1:
time: 114 us
  local copies, waits for them, and re-layouts  41.8 us (37%)
  waiting for transfers between devices  30.1 us (26%)
  starting transfers between devices  21.1 us (19%)
  between operations  13.6 us (12%)
  matrix products  6.29 us (6%)
    unnamed x15, local copies, waits for them, and re-layouts  40 us
    unnamed x2, waiting for transfers between devices  21.4 us
    ppermute x2, starting transfers between devices, with_halo(): lax.ppermute(tail, axis, [(i, (i + 1) % count) for i in range(ends)])  15.5 us
    ppermute x1, waiting for transfers between devices, per_device(): lax.ppermute(line, 'chan', [(d, (d - have) % ways) for d in range(ways)])  6.31 us
    conv_general_dilated x2, matrix products, apply_taps(): lax.conv_general_dilated(slab[None], kernel, (1, 1, 1), [(0, 0), (row_pad...  6.29 us
    ppermute x1, starting transfers between devices, per_device(): lax.ppermute(line, 'chan', [(d, (d - have) % ways) for d in range(ways)])  3.03 us
    ppermute x2, starting transfers between devices, with_halo(): lax.ppermute(head, axis, [((i + 1) % count, i) for i in range(ends)])  2.58 us
    ppermute x2, waiting for transfers between devices, with_halo(): lax.ppermute(tail, axis, [(i, (i + 1) % count) for i in range(ends)])  2.41 us
  transfers between devices with their start and end apart: 6, of which 4 were waited for; matrix products, arithmetic and copies ran while one was open for 0% of the time, Pallas kernels for 0%

profile of v1, /device:TPU:0, one launch (start us, length us, event | category | flops | bytes accessed | tf_op | source)
XLA Modules:
  0.0 113.7 jit_solution(12312533679840645471)
XLA Ops:
  6.5 0.0 copy-start
  6.5 0.0 reduce-scatter.4.cloned.1.call-start
  6.5 1.3 %copy.18 = bf16[128,1,8,128]{0,2,3,1:T(8,128)(2,1)S(1)} copy(bf16[128,1,8,128]{3,2,1,0:T(8,128)(2,1)} %param.5) | data formatting | bytes 524288 | tf_op args[0]
  7.9 3.0 %collective-permute-start = (bf16[128,1,8,128]{0,2,3,1:T(8,128)(2,1)S(1)}, bf16[128,1,8,128]{0,2,3,1:T(8,128)(2,1)S(1)}, u32[]{:S(2)}, u32[]{:S(2)}) collective-permute-start(bf16[128,1,8,128]{0,2,3,1:T(8,128)(2,1)S(1)} %copy.18), channel_id=1, source_target_pairs={{0,1},{1,0},{2,3},{3,2},{4,5},{5,4},{6,7},{7,6},{8,9},{9,8},{10,11... | collective-permute-start | bytes 786440 | tf_op jit(solution)/shard_map/ppermute | solution.py:42
  10.9 6.3 %collective-permute-done = bf16[128,1,8,128]{0,2,3,1:T(8,128)(2,1)S(1)} collective-permute-done((bf16[128,1,8,128]{0,2,3,1:T(8,128)(2,1)S(1)}, bf16[128,1,8,128]{0,2,3,1:T(8,128)(2,1)S(1)}, u32[]{:S(2)}, u32[]{:S(2)}) %collective-permute-start) | collective-permute-done | bytes 262176 | tf_op jit(solution)/shard_map/ppermute | solution.py:42
  17.2 0.4 fusion.22
  17.6 1.3 %collective-permute-start.2 = (bf16[256,1,8,128]{0,2,3,1:T(8,128)(2,1)S(1)}, bf16[256,1,8,128]{0,2,3,1:T(8,128)(2,1)S(1)}, u32[]{:S(2)}, u32[]{:S(2)}) collective-permute-start(bf16[256,1,8,128]{0,2,3,1:T(8,128)(2,1)S(1)} %fusion.22), channel_id=1, source_target_pairs={{2,0},{4,2},{6,4},{8,6},{10,8},{12,10},{14,12},{16,14},{18,16},{20... | collective-permute-start | bytes 1572872 | tf_op jit(solution)/shard_map/ppermute | solution.py:17
  18.9 3.1 %collective-permute-start.1 = (bf16[256,1,8,128]{0,2,3,1:T(8,128)(2,1)S(1)}, bf16[256,1,8,128]{0,2,3,1:T(8,128)(2,1)S(1)}, u32[]{:S(2)}, u32[]{:S(2)}) collective-permute-start(bf16[256,1,8,128]{0,2,3,1:T(8,128)(2,1)S(1)} %fusion.22), channel_id=1, source_target_pairs={{0,2},{2,4},{4,6},{6,8},{8,10},{10,12},{12,14},{14,16},{16,18},{18... | collective-permute-start | bytes 1572872 | tf_op jit(solution)/shard_map/ppermute | solution.py:15
  22.0 0.0 collective-permute-done.2
  22.0 1.5 %collective-permute-done.1 = bf16[256,1,8,128]{0,2,3,1:T(8,128)(2,1)S(1)} collective-permute-done((bf16[256,1,8,128]{0,2,3,1:T(8,128)(2,1)S(1)}, bf16[256,1,8,128]{0,2,3,1:T(8,128)(2,1)S(1)}, u32[]{:S(2)}, u32[]{:S(2)}) %collective-permute-start.1) | collective-permute-done | bytes 524320 | tf_op jit(solution)/shard_map/ppermute | solution.py:15
  23.5 0.2 maximum_bitcast_fusion
  23.7 0.1 pad
  23.8 0.0 copy-start.3
  23.8 0.0 copy-start.4
  23.8 0.3 copy.21
  24.2 1.1 copy-done.3
  25.3 0.0 copy-done.4
  25.3 0.0 copy-start.2
  25.3 4.1 %fusion.10 = f32[1,8,8,17,128]{4,2,3,1,0:T(8,128)S(1)} fusion(bf16[256,3,3,3,128]{4,0,3,2,1:T(8,128)(2,1)S(1)} %bitcast.46, bf16[256,3,8,1,7,2]{0,4,5,2,1,3:T(8,128)(2,1)S(1)} %slice.4, bf16[256,3,8,1,8,17]{0,4,5,2,1,3:T(8,128)(2,1)S(1)} %copy.21, pred[8,17]{0,1:T(8,128)(4,1)S(1)} %copy-done.4), kind=kOutput, calls=%fused_computation.13 | convolution fusion | flops 1770496000 | bytes 4169864 | tf_op jit(solution)/shard_map/conv_general_dilated | solution.py:26
  29.4 0.1 copy.22
  29.5 0.0 copy-done.2
  29.5 0.1 fusion.25
  29.6 1.3 %collective-permute-start.4 = (bf16[128,1,8,128]{0,2,3,1:T(8,128)(2,1)S(1)}, bf16[128,1,8,128]{0,2,3,1:T(8,128)(2,1)S(1)}, u32[]{:S(2)}, u32[]{:S(2)}) collective-permute-start(bf16[128,1,8,128]{0,2,3,1:T(8,128)(2,1)S(1)} %fusion.25), channel_id=1, source_target_pairs={{2,0},{4,2},{6,4},{8,6},{10,8},{12,10},{14,12},{16,14},{18,16},{20... | collective-permute-start | bytes 786440 | tf_op jit(solution)/shard_map/ppermute | solution.py:17
  30.9 12.4 %collective-permute-start.3 = (bf16[128,1,8,128]{0,2,3,1:T(8,128)(2,1)S(1)}, bf16[128,1,8,128]{0,2,3,1:T(8,128)(2,1)S(1)}, u32[]{:S(2)}, u32[]{:S(2)}) collective-permute-start(bf16[128,1,8,128]{0,2,3,1:T(8,128)(2,1)S(1)} %fusion.25), channel_id=1, source_target_pairs={{0,2},{2,4},{4,6},{6,8},{8,10},{10,12},{12,14},{14,16},{16,18},{18... | collective-permute-start | bytes 786440 | tf_op jit(solution)/shard_map/ppermute | solution.py:15
  43.3 0.0 collective-permute-done.4
  43.3 0.9 collective-permute-done.3
  44.3 0.1 maximum_bitcast_fusion.1
  44.4 0.1 pad.2
  44.4 0.1 copy.24
  44.6 0.0 copy-done
  44.6 2.2 %fusion.9 = bf16[1,8,8,17,256]{4,2,3,1,0:T(8,128)(2,1)S(1)} fusion(bf16[128,3,3,3,256]{4,0,3,2,1:T(8,128)(2,1)S(1)} %bitcast.39, bf16[128,3,8,1,7,2]{0,4,5,2,1,3:T(8,128)(2,1)S(1)} %slice.6, bf16[128,3,8,1,8,17]{0,4,5,2,1,3:T(8,128)(2,1)S(1)} %copy.24, pred[8,17]{0,1:T(8,128)(4,1)S(1)} %copy-done.4), kind=kOutput, calls=%fused_computation.12 | convolution fusion | flops 1768112128 | bytes 3248264 | tf_op jit(solution)/shard_map/conv_general_dilated | solution.py:26
  46.8 0.1 copy.25
  46.9 11.8 %copy.27 = bf16[256,1,8,128]{2,3,1,0:T(8,128)(2,1)} copy(bf16[256,1,8,128]{0,2,3,1:T(8,128)(2,1)S(1)} %slice_bitcast_fusion) | data formatting | bytes 1048576
  58.7 13.5 %reshape.71 = bf16[256,1024]{1,0:T(8,128)(2,1)} reshape(bf16[256,1,128,8]{3,2,1,0:T(8,128)(2,1)} %bitcast.40) | data formatting | bytes 1048576
  72.2 0.0 reduce-scatter.4.cloned.1.call-update
  72.2 21.4 %reduce-scatter.4.cloned.1.call-done = bf16[128,1024]{1,0:T(8,128)(2,1)} async-done(((bf16[256,1024]{1,0:T(8,128)(2,1)}), bf16[128,1024]{1,0:T(8,128)(2,1)}) %reduce-scatter.4.cloned.1.call-update) | async-done | bytes 262160
  93.6 6.8 %reshape.72 = bf16[128,1,128,8]{3,2,1,0:T(8,128)(2,1)} reshape(bf16[128,1024]{1,0:T(8,128)(2,1)} %reduce-scatter.4.cloned.1.call-done) | data formatting | bytes 524288
  100.4 0.0 copy-start.1
  100.4 5.5 %copy.28 = bf16[128,1,8,128]{0,2,3,1:T(8,128)(2,1)S(1)} copy(bf16[128,1,8,128]{2,3,1,0:T(8,128)(2,1)} %bitcast.41) | data formatting | bytes 524288
  105.9 0.0 copy-done.1
  105.9 0.1 maximum_convert_fusion
  106.0 0.9 copy.26
  (3 shorter events, 0.1 us)
Async XLA Ops:
  6.5 38.0 %copy-start = (bf16[128,27,256]{2,0,1:T(8,128)(2,1)S(1)}, bf16[128,27,256]{2,0,1:T(8,128)(2,1)}, u32[]{:S(2)}) copy-start(bf16[128,27,256]{2,0,1:T(8,128)(2,1)} %param.8) | copy-start | bytes 5308420
  6.5 87.0 %reduce-scatter.4.cloned.1.call-start = ((), (), s32[]{:S(2)}) async-start(), calls=%async_computation.1 | async-start | bytes 786432
  7.9 9.3 %collective-permute-start = (bf16[128,1,8,128]{0,2,3,1:T(8,128)(2,1)S(1)}, bf16[128,1,8,128]{0,2,3,1:T(8,128)(2,1)S(1)}, u32[]{:S(2)}, u32[]{:S(2)}) collective-permute-start(bf16[128,1,8,128]{0,2,3,1:T(8,128)(2,1)S(1)} %copy.18), channel_id=1, source_target_pairs={{0,1},{1,0},{2,3},{3,2},{4,5},{5,4},{6,7},{7,6},{8,9},{9,8},{10,11... | collective-permute-start | bytes 786440 | tf_op jit(solution)/shard_map/ppermute | solution.py:42
  17.6 4.4 %collective-permute-start.2 = (bf16[256,1,8,128]{0,2,3,1:T(8,128)(2,1)S(1)}, bf16[256,1,8,128]{0,2,3,1:T(8,128)(2,1)S(1)}, u32[]{:S(2)}, u32[]{:S(2)}) collective-permute-start(bf16[256,1,8,128]{0,2,3,1:T(8,128)(2,1)S(1)} %fusion.22), channel_id=1, source_target_pairs={{2,0},{4,2},{6,4},{8,6},{10,8},{12,10},{14,12},{16,14},{18,16},{20... | collective-permute-start | bytes 1572872 | tf_op jit(solution)/shard_map/ppermute | solution.py:17
  18.9 4.6 %collective-permute-start.1 = (bf16[256,1,8,128]{0,2,3,1:T(8,128)(2,1)S(1)}, bf16[256,1,8,128]{0,2,3,1:T(8,128)(2,1)S(1)}, u32[]{:S(2)}, u32[]{:S(2)}) collective-permute-start(bf16[256,1,8,128]{0,2,3,1:T(8,128)(2,1)S(1)} %fusion.22), channel_id=1, source_target_pairs={{0,2},{2,4},{4,6},{6,8},{8,10},{10,12},{12,14},{14,16},{16,18},{18... | collective-permute-start | bytes 1572872 | tf_op jit(solution)/shard_map/ppermute | solution.py:15
  23.8 1.5 %copy-start.3 = (bf16[256,27,128]{2,0,1:T(8,128)(2,1)S(1)}, bf16[256,27,128]{2,0,1:T(8,128)(2,1)}, u32[]{:S(2)}) copy-start(bf16[256,27,128]{2,0,1:T(8,128)(2,1)} %param.6) | copy-start | bytes 5308420
  23.8 1.5 %copy-start.4 = (pred[8,17]{0,1:T(8,128)(4,1)S(1)}, pred[8,17]{0,1:T(8,128)(4,1)}, u32[]{:S(2)}) copy-start(pred[8,17]{0,1:T(8,128)(4,1)} %constant.41) | copy-start | bytes 412
  25.3 4.2 %copy-start.2 = (f32[128]{0:T(128)S(1)}, f32[128]{0:T(128)}, u32[]{:S(2)}) copy-start(f32[128]{0:T(128)} %param.7) | copy-start | bytes 1540
  29.6 13.7 %collective-permute-start.4 = (bf16[128,1,8,128]{0,2,3,1:T(8,128)(2,1)S(1)}, bf16[128,1,8,128]{0,2,3,1:T(8,128)(2,1)S(1)}, u32[]{:S(2)}, u32[]{:S(2)}) collective-permute-start(bf16[128,1,8,128]{0,2,3,1:T(8,128)(2,1)S(1)} %fusion.25), channel_id=1, source_target_pairs={{2,0},{4,2},{6,4},{8,6},{10,8},{12,10},{14,12},{16,14},{18,16},{20... | collective-permute-start | bytes 786440 | tf_op jit(solution)/shard_map/ppermute | solution.py:17
  30.9 13.4 %collective-permute-start.3 = (bf16[128,1,8,128]{0,2,3,1:T(8,128)(2,1)S(1)}, bf16[128,1,8,128]{0,2,3,1:T(8,128)(2,1)S(1)}, u32[]{:S(2)}, u32[]{:S(2)}) collective-permute-start(bf16[128,1,8,128]{0,2,3,1:T(8,128)(2,1)S(1)} %fusion.25), channel_id=1, source_target_pairs={{0,2},{2,4},{4,6},{6,8},{8,10},{10,12},{12,14},{14,16},{16,18},{18... | collective-permute-start | bytes 786440 | tf_op jit(solution)/shard_map/ppermute | solution.py:15
  100.4 5.5 %copy-start.1 = (f32[128]{0:T(128)S(1)}, f32[128]{0:T(128)}, u32[]{:S(2)}) copy-start(f32[128]{0:T(128)} %param.9) | copy-start | bytes 1540
Sparse Core Ops, SparseCore 0:
  72.3 21.2 reduce-scatter.3
